TPU v7x, 32 devices: a whole 2x2x4 slice. The times are simulated.
32 devices in a mesh: row: 8 (over y, x, core), rep: 4 (over z).
Axes of the slice: x: 2, y: 2, z: 4, core: 2. Of those that a mesh axis runs over, the one named last changes fastest.
Arguments:
- features: bfloat16 [8192, 512], P(('row', 'rep')), may hold values from -6 to 6
- tiles: bfloat16 [64, 8, 128, 128], P(('row', 'rep')), may hold values from -0.1875 to 0.1875
- columns: int32 [64, 8], P(('row', 'rep')), may hold values from 0 to 63, as said below
- w_aggregate: bfloat16 [512, 512], replicated, may hold values from -0.25 to 0.25
- w_self: bfloat16 [512, 512], replicated, may hold values from -0.25 to 0.25
- w_middle: bfloat16 [512, 512], replicated, may hold values from -0.25 to 0.25
- w_output: bfloat16 [512, 512], replicated, may hold values from -0.25 to 0.25
- cotangent: bfloat16 [8192, 512], P(('row', 'rep')), may hold values from -6 to 6
Outputs:
- updated: bfloat16 [8192, 512], P(('row', 'rep'))
- grad_features: bfloat16 [8192, 512], P(('row', 'rep'))
- grad_output: float32 [512, 512], P('rep')
- grad_middle: float32 [512, 512], P('rep')
- grad_aggregate: float32 [512, 512], P('rep')
- grad_self: float32 [512, 512], P('rep')
Inputs may be any that keep to these rules, and one draw needn't show every extreme that they name: `columns`: row group g holds row blocks g * 8 to (g + 1) * 8 - 1, for g < 8. Every column block named by a row block of group g lies in group g - 1, g or g + 1, taken modulo 8; every row block names each of these three groups at least once. Column blocks may repeat within a row block.
All inputs are finite; a program needn't handle non-finite values.
Results may differ from a plain program's by a relative error of at most 0.015.
Values may be sent and summed in bfloat16 or wider, within the bound.
No kernel may reach another device: no remote copies, remote signals or barrier semaphores. Data moves between devices by JAX's collectives and lax.ppermute only.
A program may use at most 192 MiB of HBM per device.

v0:
```python
import math
import jax
import jax.numpy as jnp
from jax import lax
from jax.sharding import PartitionSpec as P


def from_behind(value, axis, steps):
    count = lax.axis_size(axis)
    pairs = [(source, (source + steps) % count) for source in range(count)]
    return lax.ppermute(value, axis, pairs)


def silu_slope(value):
    sig = jax.nn.sigmoid(value)
    return sig * (1.0 + value * (1.0 - sig))


def times_transposed(left_operand, weight):
    return lax.dot_general(
        left_operand, weight, (((1,), (1,)), ((), ())), preferred_element_type=jnp.float32
    )


def local(features, tiles, columns, w_aggregate, w_self, w_middle, w_output, cotangent):
    blocks_dev, width_k, tile_size, _ = tiles.shape
    width = features.shape[1]
    groups = lax.axis_size("row")
    replicas = lax.axis_size("rep")
    panel_blocks = replicas * blocks_dev
    panel_rows = panel_blocks * tile_size
    group_id = lax.axis_index("row")
    slot_of = (columns // panel_blocks - group_id + 1) % groups
    window_index = slot_of * panel_blocks + columns % panel_blocks
    own_panel = lax.all_gather(features, "rep", axis=0, tiled=True)
    prior_panel = from_behind(own_panel, "row", 1)
    next_panel = from_behind(own_panel, "row", -1)
    window = jnp.concatenate([prior_panel, own_panel, next_panel], 0).reshape(
        3 * panel_blocks, tile_size, width
    )
    picked = window[window_index]
    summed = jnp.einsum("bkij,bkjf->bif", tiles, picked, preferred_element_type=jnp.float32)
    aggregate = summed.reshape(blocks_dev * tile_size, width).astype(jnp.bfloat16)
    pre_first = jnp.dot(aggregate, w_aggregate, preferred_element_type=jnp.float32) + jnp.dot(
        features, w_self, preferred_element_type=jnp.float32
    )
    first = jax.nn.silu(pre_first).astype(jnp.bfloat16)
    pre_second = jnp.dot(first, w_middle, preferred_element_type=jnp.float32)
    second = jax.nn.silu(pre_second).astype(jnp.bfloat16)
    updated = (
        features.astype(jnp.float32) + jnp.dot(second, w_output, preferred_element_type=jnp.float32)
    ).astype(jnp.bfloat16)
    delta_second = (times_transposed(cotangent, w_output) * silu_slope(pre_second)).astype(
        jnp.bfloat16
    )
    delta_first = (times_transposed(delta_second, w_middle) * silu_slope(pre_first)).astype(
        jnp.bfloat16
    )
    delta_aggregate = times_transposed(delta_first, w_aggregate).astype(jnp.bfloat16)
    delta_blocks = delta_aggregate.reshape(blocks_dev, tile_size, width)
    messages = jnp.einsum("bkji,bjf->bkif", tiles, delta_blocks, preferred_element_type=jnp.float32)
    spread = jnp.zeros((3 * panel_blocks, tile_size, width), jnp.float32)
    spread = spread.at[window_index.reshape(-1)].add(messages.reshape(-1, tile_size, width))
    spread = spread.reshape(3 * panel_rows, width)
    prior_part = spread[:panel_rows]
    own_part = spread[panel_rows : 2 * panel_rows]
    next_part = spread[2 * panel_rows :]
    from_next = from_behind(prior_part.astype(jnp.bfloat16), "row", -1).astype(prior_part.dtype)
    from_prior = from_behind(next_part.astype(jnp.bfloat16), "row", 1).astype(next_part.dtype)
    returned = lax.psum_scatter(
        (own_part + from_next + from_prior).astype(jnp.bfloat16),
        "rep",
        scatter_dimension=0,
        tiled=True,
    ).astype(jnp.float32)
    grad_features = (
        cotangent.astype(jnp.float32) + times_transposed(delta_first, w_self) + returned
    ).astype(jnp.bfloat16)
    total_nodes = features.shape[0] * groups * replicas
    scale = 1.0 / math.sqrt(total_nodes)
    local_output = jnp.dot(second.T, cotangent, preferred_element_type=jnp.float32)
    local_middle = jnp.dot(first.T, delta_second, preferred_element_type=jnp.float32)
    local_aggregate = jnp.dot(aggregate.T, delta_first, preferred_element_type=jnp.float32)
    local_self = jnp.dot(features.T, delta_first, preferred_element_type=jnp.float32)
    shares = (
        lax.psum_scatter(
            local_output.astype(jnp.bfloat16), "rep", scatter_dimension=0, tiled=True
        ).astype(jnp.float32),
        lax.psum_scatter(
            local_middle.astype(jnp.bfloat16), "rep", scatter_dimension=0, tiled=True
        ).astype(jnp.float32),
        lax.psum_scatter(
            local_aggregate.astype(jnp.bfloat16), "rep", scatter_dimension=0, tiled=True
        ).astype(jnp.float32),
        lax.psum_scatter(
            local_self.astype(jnp.bfloat16), "rep", scatter_dimension=0, tiled=True
        ).astype(jnp.float32),
    )
    totals = (
        lax.psum(shares[0].astype(jnp.bfloat16), "row").astype(jnp.float32),
        lax.psum(shares[1].astype(jnp.bfloat16), "row").astype(jnp.float32),
        lax.psum(shares[2].astype(jnp.bfloat16), "row").astype(jnp.float32),
        lax.psum(shares[3].astype(jnp.bfloat16), "row").astype(jnp.float32),
    )
    return (
        updated,
        grad_features,
        totals[0] * scale,
        totals[1] * scale,
        totals[2] * scale,
        totals[3] * scale,
    )


def solution(mesh):
    placed = (
        P(("row", "rep"), None),
        P(("row", "rep"), None, None, None),
        P(("row", "rep"), None),
        P(),
        P(),
        P(),
        P(),
        P(("row", "rep"), None),
    )
    return jax.shard_map(
        local,
        mesh=mesh,
        in_specs=placed,
        out_specs=(
            P(("row", "rep"), None),
            P(("row", "rep"), None),
            P("rep", None),
            P("rep", None),
            P("rep", None),
            P("rep", None),
        ),
        check_vma=False,
    )
```

profile of v0, /device:TPU:0, one launch (start us, length us, event | category | flops | bytes accessed | tf_op | source)
XLA Modules:
  0.0 258.1 jit_solution(4128961649939991356)
XLA Ops:
  8.0 32.3 %all-gather.2.cloned.1.call-done = bf16[1024,512]{1,0:T(8,128)(2,1)} async-done(((bf16[256,512]{1,0:T(8,128)(2,1)}), bf16[1024,512]{1,0:T(8,128)(2,1)}) %all-gather.2.cloned.1.call-update) | async-done | bytes 1048592 | tf_op jit(solution)/shard_map/all_gather | solution.py:35
  42.4 22.6 %collective-permute-done.1 = bf16[1024,512]{1,0:T(8,128)(2,1)S(1)} collective-permute-done((bf16[1024,512]{1,0:T(8,128)(2,1)}, bf16[1024,512]{1,0:T(8,128)(2,1)S(1)}, u32[]{:S(2)}, u32[]{:S(2)}) %collective-permute-start.1) | collective-permute-done | bytes 1048608 | tf_op jit(solution)/shard_map/ppermute | solution.py:11
  65.1 1.8 collective-permute-done
  66.9 2.8 %pad_maximum_fusion = bf16[3072,512]{1,0:T(8,128)(2,1)} fusion(bf16[1024,512]{1,0:T(8,128)(2,1)S(1)} %collective-permute-done.1, bf16[1024,512]{1,0:T(8,128)(2,1)} %all-gather.2.cloned.1.call-done, bf16[1024,512]{1,0:T(8,128)(2,1)S(1)} %collective-permute-done), kind=kLoop, calls=%fused_computation.2 | loop fusion | flops 9437184 | bytes 6291456 | tf_op jit(solution)/shard_map/concatenate | solution.py:38
  69.7 2.6 gather_fusion
  76.7 1.4 fusion.6
  81.0 2.7 %fusion.15 = f32[2,512,8,128]{3,1,2,0:T(8,128)} fusion(bf16[2,128,512,1]{2,1,3,0:T(8,128)(2,1)S(1)} %bitcast.59, bf16[2,8,128,128]{3,2,1,0:T(8,128)(2,1)S(1)} %copy-done), kind=kOutput, calls=%fused_computation.49 | convolution fusion | flops 268435456 | bytes 4980736 | tf_op jit(solution)/shard_map/bkji,bjf->bkif/dot_general | solution.py:61
  83.6 5.4 %copy.15 = f32[16,128,512]{2,1,0:T(8,128)} copy(f32[16,128,512]{1,2,0:T(8,128)} %bitcast.54) | data formatting | bytes 8388608 | tf_op jit(solution)/shard_map/reshape | solution.py:63
  89.0 3.5 %broadcast_in_dim.8 = f32[24,128,512]{2,1,0:T(8,128)} broadcast(f32[]{:T(128)} %constant.53.clone.1), dimensions={} | broadcast | bytes 6291460 | tf_op jit(solution)/shard_map/broadcast_in_dim | solution.py:62
  92.5 9.6 %scatter_fusion = f32[24,128,512]{2,1,0:T(8,128)} fusion(f32[24,128,512]{2,1,0:T(8,128)} %broadcast_in_dim.8, s32[16]{0:T(128)S(1)} %fusion.10, f32[16,128,512]{2,1,0:T(8,128)} %copy.15), kind=kCustom, calls=%fused_computation.1 | custom fusion | flops 1048576 | bytes 12582976 | tf_op jit(solution)/shard_map/scatter-add | solution.py:63
  102.0 3.4 %convert.4 = bf16[24,128,512]{2,1,0:T(8,128)(2,1)S(1)} convert(f32[24,128,512]{2,1,0:T(8,128)} %scatter_fusion) | non-fusion elementwise | flops 1572864 | bytes 9437184 | tf_op jit(solution)/shard_map/convert.1
  105.4 1.6 fusion.13
  108.3 2.7 %collective-permute-start.2 = (bf16[1024,512]{1,0:T(8,128)(2,1)}, bf16[1024,512]{1,0:T(8,128)(2,1)}, u32[]{:S(2)}, u32[]{:S(2)}) collective-permute-start(bf16[1024,512]{1,0:T(8,128)(2,1)} %bitcast.12), channel_id=1, source_target_pairs={{0,28},{4,0},{8,4},{12,8},{16,12},{20,16},{24,20},{28,24},{1,29},{... | collective-permute-start | bytes 3145736 | tf_op jit(solution)/shard_map/ppermute | solution.py:11
  111.0 1.9 slice.22
  112.9 6.7 %reduce-scatter.12.cloned.1.call-done = bf16[128,512]{1,0:T(8,128)(2,1)} async-done(((bf16[512,512]{1,0:T(8,128)(2,1)}), bf16[128,512]{1,0:T(8,128)(2,1)}) %reduce-scatter.12.cloned.1.call-update) | async-done | bytes 131088 | tf_op jit(solution)/shard_map/reduce_scatter | solution.py:92
  119.5 22.2 %reduce-scatter.8.cloned.1.call-done = bf16[128,512]{1,0:T(8,128)(2,1)} async-done(((bf16[512,512]{1,0:T(8,128)(2,1)}), bf16[128,512]{1,0:T(8,128)(2,1)}) %reduce-scatter.8.cloned.1.call-update) | async-done | bytes 131088 | tf_op jit(solution)/shard_map/reduce_scatter | solution.py:86
  141.8 22.2 %reduce-scatter.14.cloned.1.call-done = bf16[128,512]{1,0:T(8,128)(2,1)} async-done(((bf16[512,512]{1,0:T(8,128)(2,1)}), bf16[128,512]{1,0:T(8,128)(2,1)}) %reduce-scatter.14.cloned.1.call-update) | async-done | bytes 131088 | tf_op jit(solution)/shard_map/reduce_scatter | solution.py:95
  164.1 3.2 %fusion.1 = bf16[1024,512]{1,0:T(8,128)(2,1)} fusion(f32[8,128,512]{2,1,0:T(8,128)S(1)} %slice.22, bf16[1024,512]{1,0:T(8,128)(2,1)} %collective-permute-done.3, bf16[1024,512]{1,0:T(8,128)(2,1)} %collective-permute-done.2), kind=kLoop, calls=%fused_computation.5 | loop fusion | flops 2621440 | bytes 5242880 | tf_op jit(solution)/shard_map/convert_element_type | solution.py:71
  167.4 2.3 fusion.4
  170.0 50.6 %all-reduce.3.cloned.1.call-done = (bf16[128,512]{1,0:T(8,128)(2,1)}, bf16[128,512]{1,0:T(8,128)(2,1)}, bf16[128,512]{1,0:T(8,128)(2,1)}, bf16[128,512]{1,0:T(8,128)(2,1)}) async-done(((bf16[128,512]{1,0:T(8,128)(2,1)}, bf16[128,512]{1,0:T(8,128)(2,1)}, bf16[128,512]{1,0:T(8,128)(2,1)}, bf16[128,512]{1,0:T(8,128)(2,1)}), (bf16[128,512]{1,0:T(8,128)(2,1)}, bf16[128,512]{1,0:T(8,128)(2,1)}, ...) | async-done | bytes 524304 | tf_op jit(solution)/shard_map/psum | solution.py:100
  220.6 1.8 convert_multiply_fusion.2
  222.4 1.8 convert_multiply_fusion
  224.2 25.3 %reduce-scatter.6.cloned.1.call-done = bf16[256,512]{1,0:T(8,128)(2,1)} async-done(((bf16[1024,512]{1,0:T(8,128)(2,1)}), bf16[256,512]{1,0:T(8,128)(2,1)}) %reduce-scatter.6.cloned.1.call-update) | async-done | bytes 262160 | tf_op jit(solution)/shard_map/reduce_scatter | solution.py:70
  249.6 1.7 add_convert_fusion
  (64 shorter events, 11.6 us)
Async XLA Ops:
  7.2 65.1 %copy-start = (bf16[2,8,128,128]{3,2,1,0:T(8,128)(2,1)S(1)}, bf16[2,8,128,128]{3,2,1,0:T(8,128)(2,1)}, u32[]{:S(2)}) copy-start(bf16[2,8,128,128]{3,2,1,0:T(8,128)(2,1)} %param.9) | copy-start | bytes 1572868
  7.2 33.1 %all-gather.2.cloned.1.call-start = ((), (), s32[]{:S(2)}) async-start(), calls=%async_computation.5 | async-start | bytes 1310720 | tf_op jit(solution)/shard_map/all_gather | solution.py:35
  7.9 104.9 %reduce-scatter.10.cloned.1.call-start = ((), (), s32[]{:S(2)}) async-start(), calls=%async_computation.8 | async-start | bytes 655360 | tf_op jit(solution)/shard_map/reduce_scatter | solution.py:89
  40.3 24.8 %collective-permute-start.1 = (bf16[1024,512]{1,0:T(8,128)(2,1)}, bf16[1024,512]{1,0:T(8,128)(2,1)S(1)}, u32[]{:S(2)}, u32[]{:S(2)}) collective-permute-start(bf16[1024,512]{1,0:T(8,128)(2,1)} %all-gather.2.cloned.1.call-done), channel_id=1, source_target_pairs={{0,28},{4,0},{8,4},{12,8},{16,12},{20,16},{24,20},{28,24},{1,29},{... | collective-permute-start | bytes 3145736 | tf_op jit(solution)/shard_map/ppermute | solution.py:11
  41.6 25.3 %collective-permute-start = (bf16[1024,512]{1,0:T(8,128)(2,1)}, bf16[1024,512]{1,0:T(8,128)(2,1)S(1)}, u32[]{:S(2)}, u32[]{:S(2)}) collective-permute-start(bf16[1024,512]{1,0:T(8,128)(2,1)} %all-gather.2.cloned.1.call-done), channel_id=1, source_target_pairs={{0,4},{4,8},{8,12},{12,16},{16,20},{20,24},{24,28},{28,0},{1,5},{5... | collective-permute-start | bytes 3145736 | tf_op jit(solution)/shard_map/ppermute | solution.py:11
  72.3 1.0 copy-start.4
  72.3 1.3 copy-start.1
  72.3 1.3 copy-start.2
  72.3 1.6 copy-start.8
  72.8 1.5 copy-start.6
  72.8 1.5 copy-start.10
  74.3 2.3 copy-start.11
  74.3 2.4 copy-start.9
  76.6 2.8 %copy-start.12 = (f32[256,512]{1,0:T(8,128)S(1)}, f32[256,512]{1,0:T(8,128)}, u32[]{:S(2)}) copy-start(f32[256,512]{1,0:T(8,128)} %copy-done.11) | copy-start | bytes 1572868
  76.6 43.0 %reduce-scatter.12.cloned.1.call-start = ((), (), s32[]{:S(2)}) async-start(), calls=%async_computation.9 | async-start | bytes 655360 | tf_op jit(solution)/shard_map/reduce_scatter | solution.py:92
  78.1 2.5 copy-start.5
  79.2 62.6 %reduce-scatter.8.cloned.1.call-start = ((), (), s32[]{:S(2)}) async-start(), calls=%async_computation.7 | async-start | bytes 655360 | tf_op jit(solution)/shard_map/reduce_scatter | solution.py:86
  80.6 83.5 %reduce-scatter.14.cloned.1.call-start = ((), (), s32[]{:S(2)}) async-start(), calls=%async_computation.10 | async-start | bytes 655360 | tf_op jit(solution)/shard_map/reduce_scatter | solution.py:95
  107.0 57.1 %collective-permute-start.3 = (bf16[1024,512]{1,0:T(8,128)(2,1)}, bf16[1024,512]{1,0:T(8,128)(2,1)}, u32[]{:S(2)}, u32[]{:S(2)}) collective-permute-start(bf16[1024,512]{1,0:T(8,128)(2,1)} %bitcast.13), channel_id=1, source_target_pairs={{0,4},{4,8},{8,12},{12,16},{16,20},{20,24},{24,28},{28,0},{1,5},{5... | collective-permute-start | bytes 3145736 | tf_op jit(solution)/shard_map/ppermute | solution.py:11
  108.2 112.4 %all-reduce.3.cloned.1.call-start = ((), (), s32[]{:S(2)}) async-start(), calls=%async_computation.11 | async-start | bytes 1048576 | tf_op jit(solution)/shard_map/psum | solution.py:100
  108.3 55.8 %collective-permute-start.2 = (bf16[1024,512]{1,0:T(8,128)(2,1)}, bf16[1024,512]{1,0:T(8,128)(2,1)}, u32[]{:S(2)}, u32[]{:S(2)}) collective-permute-start(bf16[1024,512]{1,0:T(8,128)(2,1)} %bitcast.12), channel_id=1, source_target_pairs={{0,28},{4,0},{8,4},{12,8},{16,12},{20,16},{24,20},{28,24},{1,29},{... | collective-permute-start | bytes 3145736 | tf_op jit(solution)/shard_map/ppermute | solution.py:11
  164.0 85.5 %reduce-scatter.6.cloned.1.call-start = ((), (), s32[]{:S(2)}) async-start(), calls=%async_computation.6 | async-start | bytes 1310720 | tf_op jit(solution)/shard_map/reduce_scatter | solution.py:70
  167.3 2.3 copy-start.3
  167.3 2.3 copy-start.7
  (1 other events, 0.7 us)
Sparse Core Ops, SparseCore 0:
  9.6 30.6 all-gather.1
  76.7 20.3 reduce-scatter.9
  99.4 20.0 reduce-scatter.11
  121.7 20.0 reduce-scatter.7
  143.9 20.0 reduce-scatter.13
  167.2 53.3 all-reduce.2
  222.9 26.6 reduce-scatter.5
where the time goes:
time: 259 us; the launch traced here: 258 us
  waiting for transfers between devices  185 us (71%)
  other arithmetic  25 us (10%)
  local copies, waits for them, and re-layouts  16.3 us (6%)
  between operations  14.4 us (6%)
  matrix products  13.4 us (5%)
  starting transfers between devices  4.32 us (2%)
    psum x1, waiting for transfers between devices, local(): lax.psum(shares[0].astype(jnp.bfloat16), 'row').astype(jnp.float32)  50.6 us
    all_gather x1, waiting for transfers between devices, local(): own_panel = lax.all_gather(features, 'rep', axis=0, tiled=True)  32.3 us
    reduce_scatter x1, waiting for transfers between devices, local(): lax.psum_scatter((own_part + from_next + from_prior).astype(jnp.bfloat16)...  25.3 us
    ppermute x4, waiting for transfers between devices, from_behind(): return lax.ppermute(value, axis, pairs)  24.5 us
    reduce_scatter x1, waiting for transfers between devices, local(): lax.psum_scatter(local_output.astype(jnp.bfloat16), 'rep', scatter_dimens...  22.2 us
    reduce_scatter x1, waiting for transfers between devices, local(): lax.psum_scatter(local_self.astype(jnp.bfloat16), 'rep', scatter_dimensio...  22.2 us
    scatter-add x1, other arithmetic, local(): spread.at[window_index.reshape(-1)]  9.55 us
    reduce_scatter x1, waiting for transfers between devices, local(): lax.psum_scatter(local_aggregate.astype(jnp.bfloat16), 'rep', scatter_dim...  6.68 us
  transfers between devices with their start and end apart: 11, of which 8 were waited for; matrix products, arithmetic and copies ran while one was open for 17% of the time, Pallas kernels for 0%

commit v1 on v0

--- a/solution.py
+++ b/solution.py
@@ -32,7 +32,16 @@
     group_id = lax.axis_index("row")
     slot_of = (columns // panel_blocks - group_id + 1) % groups
     window_index = slot_of * panel_blocks + columns % panel_blocks
-    own_panel = lax.all_gather(features, "rep", axis=0, tiled=True)
+    ways = lax.axis_size("rep")
+    up = [(d, (d + 1) % ways) for d in range(ways)]
+    down = [(d, (d - 1) % ways) for d in range(ways)]
+    earlier, later = ([features], [features])
+    for __2 in range(ways // 2):
+        earlier.append(lax.ppermute(earlier[-1], "rep", up))
+    for __2 in range((ways - 1) // 2):
+        later.append(lax.ppermute(later[-1], "rep", down))
+    line = jnp.concatenate([*earlier[::-1], *later[1:]], axis=0)
+    own_panel = jnp.roll(line, (lax.axis_index("rep") - ways // 2) * features.shape[0], axis=0)
     prior_panel = from_behind(own_panel, "row", 1)
     next_panel = from_behind(own_panel, "row", -1)
     window = jnp.concatenate([prior_panel, own_panel, next_panel], 0).reshape(

time: 259 us -> 250 us (0.965)
  waiting for transfers between devices: 185 us -> 170 us
  starting transfers between devices: 4.32 us -> 10.4 us
    all_gather x1 -> x0, waiting for transfers between devices: 32.3 us -> none  [local(): own_panel = lax.all_gather(features, 'rep', axis=0, tiled=True)]
    ppermute x0 -> x3, waiting for transfers between devices: none -> 17 us  [the longest x2 15.7 us: local(): earlier.append(lax.ppermute(earlier[-1], 'rep', up))]
    ppermute x0 -> x3, starting transfers between devices: none -> 6.93 us  [the longest x1 3.82 us: local(): later.append(lax.ppermute(later[-1], 'rep', down))]
  transfers between devices with their start and end apart: 11 -> 13, of which waited for: 8 -> 10; matrix products, arithmetic and copies ran while one was open for 17% -> 17% of each run, Pallas kernels for 0% -> 0%
where the time goes in v1:
time: 250 us
  waiting for transfers between devices  170 us (68%)
  other arithmetic  24.3 us (10%)
  local copies, waits for them, and re-layouts  17.7 us (7%)
  between operations  14.4 us (6%)
  matrix products  12.4 us (5%)
  starting transfers between devices  10.4 us (4%)
    psum x1, waiting for transfers between devices, local(): lax.psum(shares[0].astype(jnp.bfloat16), 'row').astype(jnp.float32)  50.6 us
    ppermute x4, waiting for transfers between devices, from_behind(): return lax.ppermute(value, axis, pairs)  25.7 us
    reduce_scatter x1, waiting for transfers between devices, local(): lax.psum_scatter((own_part + from_next + from_prior).astype(jnp.bfloat16)...  25.2 us
    reduce_scatter x1, waiting for transfers between devices, local(): lax.psum_scatter(local_output.astype(jnp.bfloat16), 'rep', scatter_dimens...  22.4 us
    reduce_scatter x1, waiting for transfers between devices, local(): lax.psum_scatter(local_self.astype(jnp.bfloat16), 'rep', scatter_dimensio...  22.2 us
    ppermute x2, waiting for transfers between devices, local(): earlier.append(lax.ppermute(earlier[-1], 'rep', up))  15.7 us
    scatter-add x1, other arithmetic, local(): spread.at[window_index.reshape(-1)]  9.5 us
    reduce_scatter x1, waiting for transfers between devices, local(): lax.psum_scatter(local_aggregate.astype(jnp.bfloat16), 'rep', scatter_dim...  7.2 us
  transfers between devices with their start and end apart: 13, of which 10 were waited for; matrix products, arithmetic and copies ran while one was open for 17% of the time, Pallas kernels for 0%

profile of v1, /device:TPU:0, one launch (start us, length us, event | category | flops | bytes accessed | tf_op | source)
XLA Modules:
  0.0 249.7 jit_solution(17049789720000088475)
XLA Ops:
  7.2 3.1 %collective-permute-start = (bf16[256,512]{1,0:T(8,128)(2,1)}, bf16[256,512]{1,0:T(8,128)(2,1)S(1)}, u32[]{:S(2)}, u32[]{:S(2)}) collective-permute-start(bf16[256,512]{1,0:T(8,128)(2,1)} %param.8), channel_id=1, source_target_pairs={{0,1},{1,2},{2,3},{3,0},{4,5},{5,6},{6,7},{7,4},{8,9},{9,10},{10,1... | collective-permute-start | bytes 786440 | tf_op jit(solution)/shard_map/ppermute | solution.py:40
  10.3 8.5 %collective-permute-done = bf16[256,512]{1,0:T(8,128)(2,1)S(1)} collective-permute-done((bf16[256,512]{1,0:T(8,128)(2,1)}, bf16[256,512]{1,0:T(8,128)(2,1)S(1)}, u32[]{:S(2)}, u32[]{:S(2)}) %collective-permute-start) | collective-permute-done | bytes 262176 | tf_op jit(solution)/shard_map/ppermute | solution.py:40
  18.9 3.8 %collective-permute-start.2 = (bf16[256,512]{1,0:T(8,128)(2,1)}, bf16[256,512]{1,0:T(8,128)(2,1)S(1)}, u32[]{:S(2)}, u32[]{:S(2)}) collective-permute-start(bf16[256,512]{1,0:T(8,128)(2,1)} %param.8), channel_id=1, source_target_pairs={{0,3},{1,0},{2,1},{3,2},{4,7},{5,4},{6,5},{7,6},{8,11},{9,8},{10,9... | collective-permute-start | bytes 786440 | tf_op jit(solution)/shard_map/ppermute | solution.py:42
  22.7 7.2 %collective-permute-done.1 = bf16[256,512]{1,0:T(8,128)(2,1)S(1)} collective-permute-done((bf16[256,512]{1,0:T(8,128)(2,1)S(1)}, bf16[256,512]{1,0:T(8,128)(2,1)S(1)}, u32[]{:S(2)}, u32[]{:S(2)}) %collective-permute-start.1) | collective-permute-done | bytes 262176 | tf_op jit(solution)/shard_map/ppermute | solution.py:40
  33.1 22.7 %collective-permute-done.4 = bf16[1024,512]{1,0:T(8,128)(2,1)S(1)} collective-permute-done((bf16[1024,512]{1,0:T(8,128)(2,1)S(1)}, bf16[1024,512]{1,0:T(8,128)(2,1)S(1)}, u32[]{:S(2)}, u32[]{:S(2)}) %collective-permute-start.4) | collective-permute-done | bytes 1048608 | tf_op jit(solution)/shard_map/ppermute | solution.py:11
  55.8 3.0 %collective-permute-done.3 = bf16[1024,512]{1,0:T(8,128)(2,1)} collective-permute-done((bf16[1024,512]{1,0:T(8,128)(2,1)S(1)}, bf16[1024,512]{1,0:T(8,128)(2,1)}, u32[]{:S(2)}, u32[]{:S(2)}) %collective-permute-start.3) | collective-permute-done | bytes 1048608 | tf_op jit(solution)/shard_map/ppermute | solution.py:11
  58.8 2.8 %pad_maximum_fusion = bf16[3072,512]{1,0:T(8,128)(2,1)} fusion(bf16[1024,512]{1,0:T(8,128)(2,1)S(1)} %collective-permute-done.4, bf16[1024,512]{1,0:T(8,128)(2,1)S(1)} %constant_dynamic-slice_fusion, bf16[1024,512]{1,0:T(8,128)(2,1)} %collective-permute-done.3), kind=kLoop, calls=%fused_computation.2 | loop fusion | flops 9437184 | bytes 6291456 | tf_op jit(solution)/shard_map/concatenate | solution.py:47
  61.6 2.6 %gather_fusion = bf16[16,128,512]{2,1,0:T(8,128)(2,1)S(1)} fusion(bf16[24,128,512]{2,1,0:T(8,128)(2,1)} %bitcast.55, s32[1024]{0:T(1024)S(1)} %pad_clamp_fusion), kind=kCustom, calls=%fused_computation | custom fusion | bytes 4194368 | tf_op jit(solution)/shard_map/gather | solution.py:50
  72.0 2.7 %fusion.15 = f32[2,512,8,128]{3,1,2,0:T(8,128)} fusion(bf16[2,128,512,1]{2,1,3,0:T(8,128)(2,1)S(1)} %bitcast.59, bf16[2,8,128,128]{3,2,1,0:T(8,128)(2,1)S(1)} %copy-done), kind=kOutput, calls=%fused_computation.58 | convolution fusion | flops 268435456 | bytes 4980736 | tf_op jit(solution)/shard_map/bkji,bjf->bkif/dot_general | solution.py:70
  74.7 5.4 %copy.15 = f32[16,128,512]{2,1,0:T(8,128)} copy(f32[16,128,512]{1,2,0:T(8,128)} %bitcast.54) | data formatting | bytes 8388608 | tf_op jit(solution)/shard_map/reshape | solution.py:72
  80.1 3.5 %broadcast_in_dim.8 = f32[24,128,512]{2,1,0:T(8,128)} broadcast(f32[]{:T(128)} %constant.82.clone.1), dimensions={} | broadcast | bytes 6291460 | tf_op jit(solution)/shard_map/broadcast_in_dim | solution.py:71
  83.5 9.5 %scatter_fusion = f32[24,128,512]{2,1,0:T(8,128)} fusion(f32[24,128,512]{2,1,0:T(8,128)} %broadcast_in_dim.8, s32[16]{0:T(128)S(1)} %fusion.10, f32[16,128,512]{2,1,0:T(8,128)} %copy.15), kind=kCustom, calls=%fused_computation.1 | custom fusion | flops 1048576 | bytes 12582976 | tf_op jit(solution)/shard_map/scatter-add | solution.py:72
  93.0 3.3 %convert.4 = bf16[24,128,512]{2,1,0:T(8,128)(2,1)S(1)} convert(f32[24,128,512]{2,1,0:T(8,128)} %scatter_fusion) | non-fusion elementwise | flops 1572864 | bytes 9437184 | tf_op jit(solution)/shard_map/convert.1
  99.3 2.7 %collective-permute-start.5 = (bf16[1024,512]{1,0:T(8,128)(2,1)}, bf16[1024,512]{1,0:T(8,128)(2,1)}, u32[]{:S(2)}, u32[]{:S(2)}) collective-permute-start(bf16[1024,512]{1,0:T(8,128)(2,1)} %bitcast.12), channel_id=1, source_target_pairs={{0,28},{4,0},{8,4},{12,8},{16,12},{20,16},{24,20},{28,24},{1,29},{... | collective-permute-start | bytes 3145736 | tf_op jit(solution)/shard_map/ppermute | solution.py:11
  102.0 1.9 slice.22
  103.9 7.2 %reduce-scatter.12.cloned.1.call-done = bf16[128,512]{1,0:T(8,128)(2,1)} async-done(((bf16[512,512]{1,0:T(8,128)(2,1)}), bf16[128,512]{1,0:T(8,128)(2,1)}) %reduce-scatter.12.cloned.1.call-update) | async-done | bytes 131088 | tf_op jit(solution)/shard_map/reduce_scatter | solution.py:101
  111.1 22.4 %reduce-scatter.8.cloned.1.call-done = bf16[128,512]{1,0:T(8,128)(2,1)} async-done(((bf16[512,512]{1,0:T(8,128)(2,1)}), bf16[128,512]{1,0:T(8,128)(2,1)}) %reduce-scatter.8.cloned.1.call-update) | async-done | bytes 131088 | tf_op jit(solution)/shard_map/reduce_scatter | solution.py:95
  133.5 22.2 %reduce-scatter.14.cloned.1.call-done = bf16[128,512]{1,0:T(8,128)(2,1)} async-done(((bf16[512,512]{1,0:T(8,128)(2,1)}), bf16[128,512]{1,0:T(8,128)(2,1)}) %reduce-scatter.14.cloned.1.call-update) | async-done | bytes 131088 | tf_op jit(solution)/shard_map/reduce_scatter | solution.py:104
  155.8 3.2 %fusion.1 = bf16[1024,512]{1,0:T(8,128)(2,1)} fusion(f32[8,128,512]{2,1,0:T(8,128)S(1)} %slice.22, bf16[1024,512]{1,0:T(8,128)(2,1)} %collective-permute-done.6, bf16[1024,512]{1,0:T(8,128)(2,1)} %collective-permute-done.5), kind=kLoop, calls=%fused_computation.5 | loop fusion | flops 2621440 | bytes 5242880 | tf_op jit(solution)/shard_map/convert_element_type | solution.py:80
  159.1 2.3 fusion.4
  161.7 50.6 %all-reduce.3.cloned.1.call-done = (bf16[128,512]{1,0:T(8,128)(2,1)}, bf16[128,512]{1,0:T(8,128)(2,1)}, bf16[128,512]{1,0:T(8,128)(2,1)}, bf16[128,512]{1,0:T(8,128)(2,1)}) async-done(((bf16[128,512]{1,0:T(8,128)(2,1)}, bf16[128,512]{1,0:T(8,128)(2,1)}, bf16[128,512]{1,0:T(8,128)(2,1)}, bf16[128,512]{1,0:T(8,128)(2,1)}), (bf16[128,512]{1,0:T(8,128)(2,1)}, bf16[128,512]{1,0:T(8,128)(2,1)}, ...) | async-done | bytes 524304 | tf_op jit(solution)/shard_map/psum | solution.py:109
  212.3 1.8 convert_multiply_fusion.2
  214.1 1.8 convert_multiply_fusion
  216.0 25.2 %reduce-scatter.6.cloned.1.call-done = bf16[256,512]{1,0:T(8,128)(2,1)} async-done(((bf16[1024,512]{1,0:T(8,128)(2,1)}), bf16[256,512]{1,0:T(8,128)(2,1)}) %reduce-scatter.6.cloned.1.call-update) | async-done | bytes 262160 | tf_op jit(solution)/shard_map/reduce_scatter | solution.py:79
  (74 shorter events, 15.9 us)
Async XLA Ops:
  7.2 57.0 %copy-start = (bf16[2,8,128,128]{3,2,1,0:T(8,128)(2,1)S(1)}, bf16[2,8,128,128]{3,2,1,0:T(8,128)(2,1)}, u32[]{:S(2)}) copy-start(bf16[2,8,128,128]{3,2,1,0:T(8,128)(2,1)} %param.9) | copy-start | bytes 1572868
  7.2 25.1 %copy-start.1 = (bf16[256,512]{1,0:T(8,128)(2,1)S(1)}, bf16[256,512]{1,0:T(8,128)(2,1)}, u32[]{:S(2)}) copy-start(bf16[256,512]{1,0:T(8,128)(2,1)} %param.8) | copy-start | bytes 786436
  7.2 96.7 %reduce-scatter.10.cloned.1.call-start = ((), (), s32[]{:S(2)}) async-start(), calls=%async_computation.7 | async-start | bytes 655360 | tf_op jit(solution)/shard_map/reduce_scatter | solution.py:98
  7.2 11.6 %collective-permute-start = (bf16[256,512]{1,0:T(8,128)(2,1)}, bf16[256,512]{1,0:T(8,128)(2,1)S(1)}, u32[]{:S(2)}, u32[]{:S(2)}) collective-permute-start(bf16[256,512]{1,0:T(8,128)(2,1)} %param.8), channel_id=1, source_target_pairs={{0,1},{1,2},{2,3},{3,0},{4,5},{5,6},{6,7},{7,4},{8,9},{9,10},{10,1... | collective-permute-start | bytes 786440 | tf_op jit(solution)/shard_map/ppermute | solution.py:40
  18.9 11.0 %collective-permute-start.1 = (bf16[256,512]{1,0:T(8,128)(2,1)S(1)}, bf16[256,512]{1,0:T(8,128)(2,1)S(1)}, u32[]{:S(2)}, u32[]{:S(2)}) collective-permute-start(bf16[256,512]{1,0:T(8,128)(2,1)S(1)} %collective-permute-done), channel_id=1, source_target_pairs={{0,1},{1,2},{2,3},{3,0},{4,5},{5,6},{6,7},{7,4},{8,9},{9,10},{10,1... | collective-permute-start | bytes 786440 | tf_op jit(solution)/shard_map/ppermute | solution.py:40
  18.9 13.3 %collective-permute-start.2 = (bf16[256,512]{1,0:T(8,128)(2,1)}, bf16[256,512]{1,0:T(8,128)(2,1)S(1)}, u32[]{:S(2)}, u32[]{:S(2)}) collective-permute-start(bf16[256,512]{1,0:T(8,128)(2,1)} %param.8), channel_id=1, source_target_pairs={{0,3},{1,0},{2,1},{3,2},{4,7},{5,4},{6,5},{7,6},{8,11},{9,8},{10,9... | collective-permute-start | bytes 786440 | tf_op jit(solution)/shard_map/ppermute | solution.py:42
  32.4 23.4 %collective-permute-start.4 = (bf16[1024,512]{1,0:T(8,128)(2,1)S(1)}, bf16[1024,512]{1,0:T(8,128)(2,1)S(1)}, u32[]{:S(2)}, u32[]{:S(2)}) collective-permute-start(bf16[1024,512]{1,0:T(8,128)(2,1)S(1)} %constant_dynamic-slice_fusion), channel_id=1, source_target_pairs={{0,28},{4,0},{8,4},{12,8},{16,12},{20,16},{24,20},{28,24},{1,29},{... | collective-permute-start | bytes 3145736 | tf_op jit(solution)/shard_map/ppermute | solution.py:11
  32.7 26.1 %collective-permute-start.3 = (bf16[1024,512]{1,0:T(8,128)(2,1)S(1)}, bf16[1024,512]{1,0:T(8,128)(2,1)}, u32[]{:S(2)}, u32[]{:S(2)}) collective-permute-start(bf16[1024,512]{1,0:T(8,128)(2,1)S(1)} %constant_dynamic-slice_fusion), channel_id=1, source_target_pairs={{0,4},{4,8},{8,12},{12,16},{16,20},{20,24},{24,28},{28,0},{1,5},{5... | collective-permute-start | bytes 3145736 | tf_op jit(solution)/shard_map/ppermute | solution.py:11
  64.2 1.0 copy-start.4
  64.2 1.3 copy-start.2
  64.7 1.2 copy-start.9
  65.6 1.0 copy-start.6
  65.6 1.1 copy-start.10
  68.7 1.7 copy-start.12
  68.7 42.4 %reduce-scatter.12.cloned.1.call-start = ((), (), s32[]{:S(2)}) async-start(), calls=%async_computation.8 | async-start | bytes 655360 | tf_op jit(solution)/shard_map/reduce_scatter | solution.py:101
  70.3 1.4 copy-start.5
  70.3 63.2 %reduce-scatter.8.cloned.1.call-start = ((), (), s32[]{:S(2)}) async-start(), calls=%async_computation.6 | async-start | bytes 655360 | tf_op jit(solution)/shard_map/reduce_scatter | solution.py:95
  71.6 84.1 %reduce-scatter.14.cloned.1.call-start = ((), (), s32[]{:S(2)}) async-start(), calls=%async_computation.9 | async-start | bytes 655360 | tf_op jit(solution)/shard_map/reduce_scatter | solution.py:104
  98.0 57.8 %collective-permute-start.6 = (bf16[1024,512]{1,0:T(8,128)(2,1)}, bf16[1024,512]{1,0:T(8,128)(2,1)}, u32[]{:S(2)}, u32[]{:S(2)}) collective-permute-start(bf16[1024,512]{1,0:T(8,128)(2,1)} %bitcast.13), channel_id=1, source_target_pairs={{0,4},{4,8},{8,12},{12,16},{16,20},{20,24},{24,28},{28,0},{1,5},{5... | collective-permute-start | bytes 3145736 | tf_op jit(solution)/shard_map/ppermute | solution.py:11
  99.2 113.1 %all-reduce.3.cloned.1.call-start = ((), (), s32[]{:S(2)}) async-start(), calls=%async_computation.10 | async-start | bytes 1048576 | tf_op jit(solution)/shard_map/psum | solution.py:109
  99.3 56.6 %collective-permute-start.5 = (bf16[1024,512]{1,0:T(8,128)(2,1)}, bf16[1024,512]{1,0:T(8,128)(2,1)}, u32[]{:S(2)}, u32[]{:S(2)}) collective-permute-start(bf16[1024,512]{1,0:T(8,128)(2,1)} %bitcast.12), channel_id=1, source_target_pairs={{0,28},{4,0},{8,4},{12,8},{16,12},{20,16},{24,20},{28,24},{1,29},{... | collective-permute-start | bytes 3145736 | tf_op jit(solution)/shard_map/ppermute | solution.py:11
  155.8 85.4 %reduce-scatter.6.cloned.1.call-start = ((), (), s32[]{:S(2)}) async-start(), calls=%async_computation.5 | async-start | bytes 1310720 | tf_op jit(solution)/shard_map/reduce_scatter | solution.py:79
  159.1 2.3 copy-start.3
  159.1 2.3 copy-start.7
  (2 other events, 1.6 us)
Sparse Core Ops, SparseCore 0:
  68.8 19.7 reduce-scatter.9
  90.9 20.1 reduce-scatter.11
  113.4 20.0 reduce-scatter.7
  135.6 20.0 reduce-scatter.13
  158.9 53.3 all-reduce.2
  214.5 26.6 reduce-scatter.5
